TPU v7x, 512 devices: a whole 4x4x16 slice. The times are simulated.
512 devices in a mesh: space: 32 (over z, core), tm: 16 (over y, x).
Axes of the slice: x: 4, y: 4, z: 16, core: 2. Of those that a mesh axis runs over, the one named last changes fastest.
Arguments:
- snapshots: bfloat16 [65536, 16384], P('space', 'tm'), may hold values from -6 to 6
- basis: bfloat16 [65536, 256], P(('space', 'tm')), may hold values from -0.0234375 to 0.0234375
- lengths: int32 [16, 64], P('tm'), may hold values from 1 to 61, as said below
- owners: int32 [16, 64], P('tm'), may hold values from 0 to 31, as said below
Outputs:
- gram_out: bfloat16 [16, 32, 392, 392], P('tm', 'space')
- target_out: bfloat16 [16, 32, 392, 256], P('tm', 'space')
Inputs may be any that keep to these rules, and one draw needn't show every extreme that they name: Each row of lengths sums to 1024. The trajectories that one owner holds in one row have 62 snapshots together at most, and in every row some owner holds exactly 62. `owners`: in every row each space index owns exactly two trajectories.
All inputs are finite; a program needn't handle non-finite values.
Results may differ from a plain program's by a relative error of at most 0.0057.
Values may be sent and summed in bfloat16 or wider, within the bound.
No kernel may reach another device: no remote copies, remote signals or barrier semaphores. Data moves between devices by JAX's collectives and lax.ppermute only.
A program may use at most 64 MiB of HBM per device.

v0:
```python
import jax
import jax.numpy as jnp
import numpy as np
from jax import lax
from jax.sharding import PartitionSpec as P

QM = 16


def slot_plan(length_row, owner_row, owner_count, capacity, snap_count):
    traj_end = jnp.cumsum(length_row)
    starts = traj_end - length_row
    snap_index = jnp.arange(snap_count, dtype=jnp.int32)
    member = (
        (snap_index[:, None] >= starts[None, :]) & (snap_index[:, None] < traj_end[None, :])
    ).astype(jnp.int32)
    snap_start = jnp.sum(member * starts[None, :], axis=1)
    snap_end = jnp.sum(member * traj_end[None, :], axis=1)
    snap_owner = jnp.sum(member * owner_row[None, :], axis=1)
    traj_index = jnp.arange(length_row.shape[0], dtype=jnp.int32)
    same_owner = owner_row[:, None] == owner_row[None, :]
    earlier = traj_index[None, :] < traj_index[:, None]
    offset = jnp.sum(jnp.where(same_owner & earlier, length_row[None, :], 0), axis=1)
    slot_index = jnp.sum(member * offset[None, :], axis=1) + snap_index - snap_start
    has_next = (snap_index + 1 < snap_end).astype(jnp.int32)
    destination = snap_owner * capacity + slot_index
    source_rows = jnp.full((owner_count * capacity,), -1, jnp.int32).at[destination].set(snap_index)
    live_rows = jnp.zeros((owner_count * capacity,), jnp.int32).at[destination].set(has_next)
    return (source_rows, live_rows)


def library(coords, live_slots, weight_scale):
    first_mode, second_mode = np.triu_indices(QM)
    products = coords[:, first_mode] * coords[:, second_mode]
    library_rows = jnp.concatenate([coords, products], axis=1).astype(jnp.bfloat16)
    successor = jnp.concatenate(
        [coords[1:], jnp.zeros((1, coords.shape[1]), jnp.float32)], axis=0
    ).astype(jnp.bfloat16)
    weighted = library_rows * live_slots[:, None].astype(jnp.bfloat16)
    dims = (((0,), (0,)), ((), ()))
    gram_matrix = (
        lax.dot_general(weighted, library_rows, dims, preferred_element_type=jnp.float32)
        * weight_scale
    )
    targets = (
        lax.dot_general(weighted, successor, dims, preferred_element_type=jnp.float32)
        * weight_scale
    )
    return (gram_matrix.astype(jnp.bfloat16), targets.astype(jnp.bfloat16))


def on_device(snapshots, basis, lengths, owners):
    dims = (((0,), (0,)), ((), ()))
    snap_count = snapshots.shape[1]
    gathered = lax.all_gather(basis, "tm", axis=0, tiled=True)
    partial_value = lax.dot_general(snapshots, gathered, dims, preferred_element_type=jnp.float32)
    owner_count = lax.axis_size("space")
    capacity = 2 * snap_count // owner_count - 2
    source_rows, live_rows = slot_plan(lengths[0], owners[0], owner_count, capacity, snap_count)
    own_index = lax.axis_index("space")
    mine = lax.dynamic_slice_in_dim(source_rows, own_index * capacity, capacity)
    summed = lax.psum(partial_value, "space")
    packed = jnp.take(summed, jnp.maximum(mine, 0), axis=0) * (mine >= 0)[:, None].astype(
        jnp.float32
    )
    live_slots = lax.dynamic_slice_in_dim(live_rows, own_index * capacity, capacity)
    gram_matrix, targets = library(packed, live_slots, owner_count / snap_count)
    return (gram_matrix[None, None], targets[None, None])


def solution(mesh):
    placed = (P("space", "tm"), P(("space", "tm"), None), P("tm", None), P("tm", None))
    return jax.shard_map(
        on_device,
        mesh=mesh,
        in_specs=placed,
        out_specs=(P("tm", "space", None, None), P("tm", "space", None, None)),
        check_vma=False,
    )
```

profile of v0, /device:TPU:1, one launch (start us, length us, event | category | flops | bytes accessed | tf_op | source)
XLA Modules:
  0.0 301.7 jit_solution(7914927873324652971)
XLA Ops:
  7.2 0.0 all-gather.2.cloned.1.call-start
  7.2 0.7 all-gather.2.cloned.1.call-update
  7.9 0.0 all-reduce.3.cloned.1.call-start
  7.9 0.7 copy.20
  8.7 0.1 reduce-window.4
  8.8 0.1 reduce
  8.9 0.9 select_reduce_fusion.4
  9.8 0.7 fusion.17
  10.5 0.8 select_reduce_fusion
  11.4 4.3 %scatter_custom_fusion.1 = s32[1984]{0:T(1024)S(1)} fusion(s32[1024]{0:T(1024)S(1)} %bitcast.28, s32[1024]{0:T(1024)S(1)} %fusion.16, s32[]{:T(128)} %constant.22.clone.1), kind=kCustom, calls=%fused_computation.35 | custom fusion | bytes 7940 | tf_op jit(solution)/shard_map/scatter | solution.py:28
  15.7 4.3 %scatter_custom_fusion = s32[1984]{0:T(1024)S(1)} fusion(s32[1024]{0:T(1024)S(1)} %bitcast.29, s32[1024]{0:T(1024)S(1)} %iota.19, s32[]{:T(128)} %constant.21.clone.1), kind=kCustom, calls=%fused_computation.37 | custom fusion | bytes 7940 | tf_op jit(solution)/shard_map/scatter | solution.py:27
  20.0 0.0 copy-start.1
  20.1 0.0 copy-start
  20.1 52.9 %all-gather.2.cloned.1.call-done = bf16[2048,256]{1,0:T(8,128)(2,1)} async-done(((bf16[128,256]{1,0:T(8,128)(2,1)}), bf16[2048,256]{1,0:T(8,128)(2,1)}) %all-gather.2.cloned.1.call-update) | async-done | bytes 1048592 | tf_op jit(solution)/shard_map/all_gather | solution.py:55
  72.9 4.8 %fusion.22 = f32[1024,256]{1,0:T(8,128)} fusion(bf16[2048,1024]{1,0:T(8,128)(2,1)} %param.8, bf16[2048,256]{1,0:T(8,128)(2,1)} %all-gather.2.cloned.1.call-done), kind=kOutput, calls=%fused_computation.51 | convolution fusion | flops 1073741824 | bytes 6291456 | tf_op jit(solution)/shard_map/dot_general | solution.py:56
  77.7 0.0 all-reduce.3.cloned.1.call-update
  77.7 0.1 dynamic-slice_convert_fusion
  77.8 0.1 broadcast_compare_fusion
  77.9 0.0 copy-done.1
  77.9 0.0 copy-done
  77.9 211.2 %all-reduce.3.cloned.1.call-done = f32[1024,256]{1,0:T(8,128)} async-done(((f32[1024,256]{1,0:T(8,128)}), f32[1024,256]{1,0:T(8,128)}) %all-reduce.3.cloned.1.call-update) | async-done | bytes 1048592 | tf_op jit(solution)/shard_map/psum | solution.py:62
  289.2 1.9 gather_fusion
  291.0 0.1 fusion.21
  291.1 0.1 copy.21
  291.2 0.7 gather_fusion.2
  291.9 0.7 gather_fusion.1
  292.6 0.1 copy.23
  292.7 0.1 copy.24
  292.8 1.1 fusion.1
  293.9 1.0 fusion.3
  (9 shorter events, 0.1 us)
Async XLA Ops:
  7.2 65.8 %all-gather.2.cloned.1.call-start = ((), (), s32[]{:S(2)}) async-start(), calls=%async_computation | async-start | bytes 1114112 | tf_op jit(solution)/shard_map/all_gather | solution.py:55
  7.9 281.3 %all-reduce.3.cloned.1.call-start = ((), (), s32[]{:S(2)}) async-start(), calls=%async_computation.1 | async-start | bytes 2097152 | tf_op jit(solution)/shard_map/psum | solution.py:62
  20.0 57.8 %copy-start.1 = (s32[136]{0:T(256)S(1)}, s32[136]{0:T(256)}, u32[]{:S(2)}) copy-start(s32[136]{0:T(256)} %constant.68) | copy-start | bytes 1636
  20.1 57.8 %copy-start = (s32[136]{0:T(256)S(1)}, s32[136]{0:T(256)}, u32[]{:S(2)}) copy-start(s32[136]{0:T(256)} %constant.69) | copy-start | bytes 1636
Sparse Core Ops, SparseCore 0:
  11.0 61.8 all-gather.1
  77.8 211.2 all-reduce.2
where the time goes:
time: 302 us
  waiting for transfers between devices  265 us (88%)
  between operations  14.2 us (5%)
  local copies, waits for them, and re-layouts  12.9 us (4%)
  matrix products  6.86 us (2%)
    psum x1, waiting for transfers between devices, on_device(): summed = lax.psum(partial_value, 'space')  211 us
    all_gather x1, waiting for transfers between devices, on_device(): gathered = lax.all_gather(basis, 'tm', axis=0, tiled=True)  52.9 us
  transfers between devices with their start and end apart: 2, of which 2 were waited for; matrix products, arithmetic and copies ran while one was open for 4% of the time, Pallas kernels for 0%

commit v1 on v0

--- a/solution.py
+++ b/solution.py
@@ -59,7 +59,9 @@
     source_rows, live_rows = slot_plan(lengths[0], owners[0], owner_count, capacity, snap_count)
     own_index = lax.axis_index("space")
     mine = lax.dynamic_slice_in_dim(source_rows, own_index * capacity, capacity)
-    summed = lax.psum(partial_value, "space")
+    summed = partial_value
+    for hop in (1, 2, 4, 8, 16):
+        summed = summed + lax.ppermute(summed, "space", [(dev, dev ^ hop) for dev in range(32)])
     packed = jnp.take(summed, jnp.maximum(mine, 0), axis=0) * (mine >= 0)[:, None].astype(
         jnp.float32
     )

time: 302 us -> 363 us (1.20)
  the two profiles are of different devices: /device:TPU:1 before, /device:TPU:97 now
where the time goes in v1:
time: 363 us; the launch traced here: 362 us
  waiting for transfers between devices  307 us (85%)
  starting transfers between devices  22.8 us (6%)
  between operations  14.3 us (4%)
  local copies, waits for them, and re-layouts  11 us (3%)
  matrix products  5.86 us (2%)
    ppermute x5, waiting for transfers between devices, on_device(): lax.ppermute(summed, 'space', [(dev, dev ^ hop) for dev in range(32)])  243 us
    all_gather x1, waiting for transfers between devices, on_device(): gathered = lax.all_gather(basis, 'tm', axis=0, tiled=True)  63.1 us
    ppermute x5, starting transfers between devices, on_device(): lax.ppermute(summed, 'space', [(dev, dev ^ hop) for dev in range(32)])  22.8 us
  transfers between devices with their start and end apart: 6, of which 6 were waited for; matrix products, arithmetic and copies ran while one was open for 3% of the time, Pallas kernels for 0%

profile of v1, /device:TPU:97, one launch (start us, length us, event | category | flops | bytes accessed | tf_op | source)
XLA Modules:
  0.0 362.5 jit_solution(2595210567918052577)
XLA Ops:
  7.2 0.7 all-gather.2.cloned.1.call-update
  7.9 63.1 %all-gather.2.cloned.1.call-done = bf16[2048,256]{1,0:T(8,128)(2,1)} async-done(((bf16[128,256]{1,0:T(8,128)(2,1)}), bf16[2048,256]{1,0:T(8,128)(2,1)}) %all-gather.2.cloned.1.call-update) | async-done | bytes 1048592 | tf_op jit(solution)/shard_map/all_gather | solution.py:55
  71.0 3.8 %fusion.22 = f32[1024,256]{1,0:T(8,128)S(1)} fusion(bf16[2048,1024]{1,0:T(8,128)(2,1)} %param.8, bf16[2048,256]{1,0:T(8,128)(2,1)} %all-gather.2.cloned.1.call-done), kind=kOutput, calls=%fused_computation.51 | convolution fusion | flops 1073741824 | bytes 6291456 | tf_op jit(solution)/shard_map/dot_general | solution.py:56
  74.8 4.0 %collective-permute-start = (f32[1024,256]{1,0:T(8,128)S(1)}, f32[1024,256]{1,0:T(8,128)S(1)}, u32[]{:S(2)}, u32[]{:S(2)}) collective-permute-start(f32[1024,256]{1,0:T(8,128)S(1)} %fusion.22), channel_id=1, source_target_pairs={{0,16},{16,0},{32,48},{48,32},{64,80},{80,64},{96,112},{112,96},{1... | collective-permute-start | bytes 3145736 | tf_op jit(solution)/shard_map/ppermute | solution.py:64
  78.8 2.3 collective-permute-done
  81.1 0.1 add.72
  81.3 2.1 collective-permute-start.1
  83.4 24.2 %collective-permute-done.1 = f32[1024,256]{1,0:T(8,128)S(1)} collective-permute-done((f32[1024,256]{1,0:T(8,128)S(1)}, f32[1024,256]{1,0:T(8,128)S(1)}, u32[]{:S(2)}, u32[]{:S(2)}) %collective-permute-start.1) | collective-permute-done | bytes 1048608 | tf_op jit(solution)/shard_map/ppermute | solution.py:64
  107.5 0.1 add.73
  107.7 2.0 collective-permute-start.2
  109.7 48.2 %collective-permute-done.2 = f32[1024,256]{1,0:T(8,128)S(1)} collective-permute-done((f32[1024,256]{1,0:T(8,128)S(1)}, f32[1024,256]{1,0:T(8,128)S(1)}, u32[]{:S(2)}, u32[]{:S(2)}) %collective-permute-start.2) | collective-permute-done | bytes 1048608 | tf_op jit(solution)/shard_map/ppermute | solution.py:64
  157.9 0.1 add.74
  158.1 7.4 %collective-permute-start.3 = (f32[1024,256]{1,0:T(8,128)S(1)}, f32[1024,256]{1,0:T(8,128)S(1)}, u32[]{:S(2)}, u32[]{:S(2)}) collective-permute-start(f32[1024,256]{1,0:T(8,128)S(1)} %add.74), channel_id=1, source_target_pairs={{0,128},{16,144},{32,160},{48,176},{64,192},{80,208},{96,224},{112... | collective-permute-start | bytes 3145736 | tf_op jit(solution)/shard_map/ppermute | solution.py:64
  165.4 0.1 copy.20
  165.6 0.1 reduce
  165.7 0.2 select_reduce_fusion.4
  165.9 0.2 select_reduce_fusion
  166.1 108.3 %collective-permute-done.3 = f32[1024,256]{1,0:T(8,128)S(1)} collective-permute-done((f32[1024,256]{1,0:T(8,128)S(1)}, f32[1024,256]{1,0:T(8,128)S(1)}, u32[]{:S(2)}, u32[]{:S(2)}) %collective-permute-start.3) | collective-permute-done | bytes 1048608 | tf_op jit(solution)/shard_map/ppermute | solution.py:64
  274.5 0.1 add.75
  274.6 7.3 %collective-permute-start.4 = (f32[1024,256]{1,0:T(8,128)S(1)}, f32[1024,256]{1,0:T(8,128)S(1)}, u32[]{:S(2)}, u32[]{:S(2)}) collective-permute-start(f32[1024,256]{1,0:T(8,128)S(1)} %add.75), channel_id=1, source_target_pairs={{0,256},{16,272},{32,288},{48,304},{64,320},{80,336},{96,352},{112... | collective-permute-start | bytes 3145736 | tf_op jit(solution)/shard_map/ppermute | solution.py:64
  282.0 4.3 %scatter_custom_fusion.1 = s32[1984]{0:T(1024)S(1)} fusion(s32[1024]{0:T(1024)S(1)} %bitcast.26, s32[1024]{0:T(1024)S(1)} %fusion.16, s32[]{:T(128)} %constant.22.clone.1), kind=kCustom, calls=%fused_computation.35 | custom fusion | bytes 7940 | tf_op jit(solution)/shard_map/scatter | solution.py:28
  286.3 4.3 %scatter_custom_fusion = s32[1984]{0:T(1024)S(1)} fusion(s32[1024]{0:T(1024)S(1)} %bitcast.27, s32[1024]{0:T(1024)S(1)} %iota.19, s32[]{:T(128)} %constant.21.clone.1), kind=kCustom, calls=%fused_computation.37 | custom fusion | bytes 7940 | tf_op jit(solution)/shard_map/scatter | solution.py:27
  290.8 60.1 %collective-permute-done.4 = f32[1024,256]{1,0:T(8,128)S(1)} collective-permute-done((f32[1024,256]{1,0:T(8,128)S(1)}, f32[1024,256]{1,0:T(8,128)S(1)}, u32[]{:S(2)}, u32[]{:S(2)}) %collective-permute-start.4) | collective-permute-done | bytes 1048608 | tf_op jit(solution)/shard_map/ppermute | solution.py:64
  351.0 0.1 add.76
  351.1 0.7 gather_fusion
  351.9 0.1 copy.21
  352.0 0.7 gather_fusion.1
  352.6 0.1 copy.23
  352.7 0.7 gather_fusion.2
  353.4 0.1 copy.24
  353.5 1.1 fusion.1
  354.6 1.0 fusion.3
  (23 shorter events, 0.5 us)
Async XLA Ops:
  7.2 63.9 %all-gather.2.cloned.1.call-start = ((), (), s32[]{:S(2)}) async-start(), calls=%async_computation | async-start | bytes 1114112 | tf_op jit(solution)/shard_map/all_gather | solution.py:55
  74.8 90.6 %copy-start.1 = (s32[1,64]{1,0:T(1,128)S(1)}, s32[1,64]{1,0:T(1,128)}, u32[]{:S(2)}) copy-start(s32[1,64]{1,0:T(1,128)} %param.10) | copy-start | bytes 772
  74.8 90.9 %copy-start = (s32[1,64]{1,0:T(1,128)S(1)}, s32[1,64]{1,0:T(1,128)}, u32[]{:S(2)}) copy-start(s32[1,64]{1,0:T(1,128)} %param.11) | copy-start | bytes 772
  74.8 6.3 %collective-permute-start = (f32[1024,256]{1,0:T(8,128)S(1)}, f32[1024,256]{1,0:T(8,128)S(1)}, u32[]{:S(2)}, u32[]{:S(2)}) collective-permute-start(f32[1024,256]{1,0:T(8,128)S(1)} %fusion.22), channel_id=1, source_target_pairs={{0,16},{16,0},{32,48},{48,32},{64,80},{80,64},{96,112},{112,96},{1... | collective-permute-start | bytes 3145736 | tf_op jit(solution)/shard_map/ppermute | solution.py:64
  81.2 209.6 %copy-start.3 = (s32[136]{0:T(256)S(1)}, s32[136]{0:T(256)}, u32[]{:S(2)}) copy-start(s32[136]{0:T(256)} %constant.68) | copy-start | bytes 1636
  81.2 209.6 %copy-start.2 = (s32[136]{0:T(256)S(1)}, s32[136]{0:T(256)}, u32[]{:S(2)}) copy-start(s32[136]{0:T(256)} %constant.69) | copy-start | bytes 1636
  81.3 26.3 %collective-permute-start.1 = (f32[1024,256]{1,0:T(8,128)S(1)}, f32[1024,256]{1,0:T(8,128)S(1)}, u32[]{:S(2)}, u32[]{:S(2)}) collective-permute-start(f32[1024,256]{1,0:T(8,128)S(1)} %add.72), channel_id=1, source_target_pairs={{0,32},{16,48},{32,0},{48,16},{64,96},{80,112},{96,64},{112,80},{1... | collective-permute-start | bytes 3145736 | tf_op jit(solution)/shard_map/ppermute | solution.py:64
  107.7 50.3 %collective-permute-start.2 = (f32[1024,256]{1,0:T(8,128)S(1)}, f32[1024,256]{1,0:T(8,128)S(1)}, u32[]{:S(2)}, u32[]{:S(2)}) collective-permute-start(f32[1024,256]{1,0:T(8,128)S(1)} %add.73), channel_id=1, source_target_pairs={{0,64},{16,80},{32,96},{48,112},{64,0},{80,16},{96,32},{112,48},{1... | collective-permute-start | bytes 3145736 | tf_op jit(solution)/shard_map/ppermute | solution.py:64
  158.1 116.4 %collective-permute-start.3 = (f32[1024,256]{1,0:T(8,128)S(1)}, f32[1024,256]{1,0:T(8,128)S(1)}, u32[]{:S(2)}, u32[]{:S(2)}) collective-permute-start(f32[1024,256]{1,0:T(8,128)S(1)} %add.74), channel_id=1, source_target_pairs={{0,128},{16,144},{32,160},{48,176},{64,192},{80,208},{96,224},{112... | collective-permute-start | bytes 3145736 | tf_op jit(solution)/shard_map/ppermute | solution.py:64
  274.6 76.4 %collective-permute-start.4 = (f32[1024,256]{1,0:T(8,128)S(1)}, f32[1024,256]{1,0:T(8,128)S(1)}, u32[]{:S(2)}, u32[]{:S(2)}) collective-permute-start(f32[1024,256]{1,0:T(8,128)S(1)} %add.75), channel_id=1, source_target_pairs={{0,256},{16,272},{32,288},{48,304},{64,320},{80,336},{96,352},{112... | collective-permute-start | bytes 3145736 | tf_op jit(solution)/shard_map/ppermute | solution.py:64
Sparse Core Ops, SparseCore 0:
  11.0 59.9 all-gather.1
